TPU v7x, 128 devices: a whole 4x4x4 slice. The times are simulated.
128 devices in a mesh: slab: 16 (over x, y_hi, core), tile: 8 (over y_lo, z).
Axes of the slice: x: 4, y: 4 (y_hi: 2, y_lo: 2; y = y_hi * 2 + y_lo), z: 4, core: 2. Of those that a mesh axis runs over, the one named last changes fastest.
Arguments:
- velocity: float32 [3, 512, 128, 128], P(None, 'slab', 'tile'), may hold values from -4 to 4
- viscosity: float32 [512, 128, 128], P('slab', 'tile'), may hold values from 0.2 to 0.6
- basis: bfloat16 [32, 3, 512, 128, 128], P(None, None, ('slab', 'tile')), may hold values from -6 to 6
- sigma: float32 [32], replicated, may hold values from 0.3 to 3
- rotation: float32 [35, 32], replicated, may hold values from -1 to 1
Outputs:
- advanced: float32 [3, 512, 128, 128], P(None, 'slab', 'tile')
- r_factor: float32 [35, 35], replicated
- new_basis: bfloat16 [32, 3, 512, 128, 128], P(None, None, ('slab', 'tile'))
All inputs are finite; a program needn't handle non-finite values.
Results may differ from a plain program's by a relative error of at most 0.001.
Values sent between devices are 32-bit elements; how exact they have to be, the bound alone decides.
A program may use at most 256 MiB of HBM per device.

v0:
```python
import math
import jax
import jax.numpy as jnp
from jax import lax
from jax.sharding import PartitionSpec as P

step_size = 0.25


def extended(block, sides, width):
    for axis, dim in sides:
        count = lax.axis_size(axis)
        forward = [(i, i + 1) for i in range(count - 1)]
        forward.append((count - 1, 0))
        backward = [(target, source) for source, target in forward]
        low = lax.ppermute(
            lax.slice_in_dim(block, block.shape[dim] - width, None, axis=dim), axis, forward
        )
        high = lax.ppermute(lax.slice_in_dim(block, 0, width, axis=dim), axis, backward)
        block = jnp.concatenate([low, block, high], axis=dim)
    return block


def upper_factor(gram):
    order = gram.shape[0]
    positions = jnp.arange(order)
    factor = jnp.zeros_like(gram)
    for column_index in range(order):
        above = factor[:, column_index]
        remainder = gram[column_index] - jnp.dot(
            above, factor, precision=lax.Precision.HIGHEST, preferred_element_type=jnp.float32
        )
        pivot = jnp.sqrt(remainder[column_index])
        new_row = jnp.where(positions >= column_index, remainder / pivot, 0.0)
        factor = factor.at[column_index].set(new_row)
    return factor


def upper_solve(factor, right_hand):
    order = factor.shape[0]
    solved = jnp.zeros_like(right_hand)
    for row_index in range(order - 1, -1, -1):
        partial_sum = jnp.dot(
            factor[row_index],
            solved,
            precision=lax.Precision.HIGHEST,
            preferred_element_type=jnp.float32,
        )
        solved = solved.at[row_index].set(
            (right_hand[row_index] - partial_sum) / factor[row_index, row_index]
        )
    return solved


def advance(padded, viscosity):
    centre = padded[:, 1:-1, 1:-1, :]
    forward_x = padded[:, 2:, 1:-1, :]
    backward_x = padded[:, :-2, 1:-1, :]
    forward_z = padded[:, 1:-1, 2:, :]
    backward_z = padded[:, 1:-1, :-2, :]
    walled = jnp.pad(centre, ((0, 0), (0, 0), (0, 0), (1, 1)))
    above_y = walled[..., 2:]
    below_y = walled[..., :-2]
    laplace = forward_x + backward_x + forward_z + backward_z + above_y + below_y - 6.0 * centre
    carried = (
        centre[0:1] * (forward_x - backward_x)
        + centre[1:2] * (above_y - below_y)
        + centre[2:3] * (forward_z - backward_z)
    )
    return centre + step_size * (viscosity * laplace - 0.5 * carried)


def shards(velocity, viscosity, basis, sigma, rotation):
    current = velocity
    history = [velocity]
    for repeat in range(2):
        padded = extended(current, (("slab", 1), ("tile", 2)), 1)
        current = advance(padded, viscosity)
        history.append(current)
    snapshots = lax.all_to_all(jnp.stack(history), "tile", split_axis=2, concat_axis=3, tiled=True)
    strip_width = basis.shape[2]
    row_count = (
        3
        * strip_width
        * lax.axis_size("slab")
        * lax.axis_size("tile")
        * basis.shape[3]
        * basis.shape[4]
    )
    row_scale = math.sqrt(row_count)
    width_all = sigma.shape[0] + 3
    scaled = basis.astype(jnp.float32) * sigma[:, None, None, None, None]
    columns = jnp.concatenate([scaled, snapshots], 0).reshape(width_all, -1)
    local_gram = jnp.dot(
        columns, columns.T, precision=lax.Precision.HIGHEST, preferred_element_type=jnp.float32
    )
    gram = lax.psum(local_gram, ("slab", "tile"))
    factor = upper_factor(gram)
    mixing = upper_solve(factor, rotation) * row_scale
    rotated = jnp.dot(
        mixing.T, columns, precision=lax.Precision.HIGHEST, preferred_element_type=jnp.float32
    )
    rotated = rotated.reshape(basis.shape).astype(jnp.bfloat16)
    return (current, factor / row_scale, rotated)


def solution(mesh):
    in_specs = (
        P(None, "slab", "tile", None),
        P("slab", "tile", None),
        P(None, None, ("slab", "tile"), None, None),
        P(),
        P(),
    )
    out_specs = (P(None, "slab", "tile", None), P(), P(None, None, ("slab", "tile"), None, None))
    return jax.shard_map(shards, mesh=mesh, in_specs=in_specs, out_specs=out_specs, check_vma=False)
```

profile of v0, /device:TPU:1, one launch (start us, length us, event | category | flops | bytes accessed | tf_op | source)
XLA Modules:
  0.0 461.0 jit_solution(1416673244914366114)
XLA Ops:
  1.4 4.3 collective-permute-start.1
  7.9 2.6 collective-permute-done
  10.5 3.9 collective-permute-start.2
  16.8 2.7 collective-permute-done.3
  19.6 1.8 multiply_add_fusion.1
  21.4 3.4 collective-permute-start.5
  25.7 4.1 collective-permute-done.4
  32.9 2.2 collective-permute-done.7
  35.1 1.8 fusion.306
  36.9 1.6 pad_maximum_fusion.1
  38.6 3.8 all-to-all-start
  42.4 11.8 %convert_multiply_fusion = f32[32,3,4,128,128]{4,0,3,2,1:T(8,128)S(1)} fusion(bf16[32,3,4,128,128]{4,3,2,1,0:T(8,128)(2,1)} %param.147, f32[32]{0:T(128)} %param.148), kind=kLoop, calls=%fused_computation.8 | loop fusion | flops 12582912 | bytes 37748864 | tf_op jit(solution)/shard_map/mul | solution.py:92
  54.1 28.1 %copy.82 = f32[32,3,4,128,128]{4,3,2,1,0:T(8,128)} copy(f32[32,3,4,128,128]{4,0,3,2,1:T(8,128)S(1)} %convert_multiply_fusion) | data formatting | bytes 50331648 | tf_op jit(solution)/shard_map/mul | solution.py:92
  82.3 25.1 %copy.100 = f32[4,8,1536,128]{3,1,2,0:T(8,128)} copy(f32[4,8,1536,128]{3,2,1,0:T(8,128)} %bitcast.1128) | data formatting | bytes 50331648
  113.0 3.0 copy.46
  116.0 28.8 %fusion.9 = f32[35,35]{1,0:T(8,128)S(1)} fusion(f32[3,3,4,128,128]{4,0,3,2,1:T(4,128)S(1)} %bitcast.1130, f32[32,3,4,128,128]{4,0,3,2,1:T(8,128)} %copy-done.1), kind=kOutput, calls=%fused_computation.15 | convolution fusion | flops 2897018880 | bytes 27530020 | tf_op jit(solution)/shard_map/dot_general | solution.py:94
  144.8 68.9 %psum.7 = f32[35,35]{1,0:T(8,128)S(1)} all-reduce(f32[35,35]{1,0:T(8,128)S(1)} %fusion.9), channel_id=1, replica_groups=mesh['slab'=16,'tile'=8] {'slab','tile'}, use_global_device_ids=true, to_apply=%region_0.1 | all-reduce | flops 1225 | bytes 9800 | tf_op jit(solution)/shard_map/psum | solution.py:97
  299.7 1.5 fusion.89
  331.7 1.5 fusion.127
  353.6 10.1 %pad_maximum_fusion = f32[35,196608]{1,0:T(8,128)S(1)} fusion(f32[3,196608]{1,0:T(4,128)S(1)} %bitcast.1131, f32[32,196608]{1,0:T(8,128)} %bitcast.1127), kind=kLoop, calls=%fused_computation.4 | loop fusion | flops 6881280 | bytes 55050240 | tf_op jit(solution)/shard_map/concatenate | solution.py:93
  363.7 14.4 %copy.89 = f32[5,8,1536,128]{3,2,1,0:T(8,128)} copy(f32[5,8,1536,128]{3,1,2,0:T(8,128)S(1)} %bitcast.1125) | data formatting | bytes 62914560
  378.1 20.3 %slice.2142 = f32[35,1536,128]{2,1,0:T(8,128)} slice(f32[40,1536,128]{2,1,0:T(8,128)} %bitcast.1126), slice={[0:35], [0:1536], [0:128]} | slice | bytes 55050240
  398.3 48.0 %fusion.6 = bf16[32,3,4,128,128]{4,0,3,2,1:T(8,128)(2,1)S(1)} fusion(f32[3,4,128,128,35]{3,2,1,0,4:T(8,128)} %bitcast.1124, f32[35,32]{0,1:T(8,128)S(1)} %scatter.349), kind=kOutput, calls=%fused_computation.9 | convolution fusion | flops 2648704000 | bytes 40112512 | tf_op jit(solution)/shard_map/dot_general | solution.py:100
  446.4 14.5 %copy.85 = bf16[32,3,4,128,128]{4,3,2,1,0:T(8,128)(2,1)} copy(bf16[32,3,4,128,128]{4,0,3,2,1:T(8,128)(2,1)S(1)} %fusion.6) | data formatting | bytes 25165824
  (376 shorter events, 127.1 us)
Async XLA Ops:
  1.4 5.3 %collective-permute-start.1 = (f32[3,1,16,128]{3,2,0,1:T(8,128)S(1)}, f32[3,1,16,128]{3,2,0,1:T(8,128)S(1)}, u32[]{:S(2)}, u32[]{:S(2)}) collective-permute-start(f32[3,1,16,128]{3,2,0,1:T(8,128)S(1)} %get-tuple-element.905), channel_id=1, source_target_pairs={{0,8},{8,16},{16,24},{24,32},{32,40},{40,48},{48,56},{56,64},{64,7... | collective-permute-start | bytes 73736 | tf_op jit(solution)/shard_map/ppermute | solution.py:16
  5.7 4.8 %collective-permute-start = (f32[3,1,16,128]{3,2,0,1:T(8,128)S(1)}, f32[3,1,16,128]{3,2,0,1:T(8,128)S(1)}, u32[]{:S(2)}, u32[]{:S(2)}) collective-permute-start(f32[3,1,16,128]{3,2,0,1:T(8,128)S(1)} %get-tuple-element.904), channel_id=1, source_target_pairs={{8,0},{16,8},{24,16},{32,24},{40,32},{48,40},{56,48},{64,56},{72,6... | collective-permute-start | bytes 73736 | tf_op jit(solution)/shard_map/ppermute | solution.py:19
  10.5 6.3 %collective-permute-start.2 = (f32[3,34,1,128]{3,2,0,1:T(1,128)S(1)}, f32[3,34,1,128]{3,2,0,1:T(1,128)S(1)}, u32[]{:S(2)}, u32[]{:S(2)}) collective-permute-start(f32[3,34,1,128]{3,2,0,1:T(1,128)S(1)} %get-tuple-element.892), channel_id=1, source_target_pairs={{1,0},{2,1},{3,2},{4,3},{5,4},{6,5},{7,6},{0,7},{9,8},{10,9},{11,1... | collective-permute-start | bytes 156680 | tf_op jit(solution)/shard_map/ppermute | solution.py:19
  14.5 5.1 %collective-permute-start.3 = (f32[3,34,1,128]{3,2,0,1:T(1,128)S(1)}, f32[3,34,1,128]{3,2,0,1:T(1,128)S(1)}, u32[]{:S(2)}, u32[]{:S(2)}) collective-permute-start(f32[3,34,1,128]{3,2,0,1:T(1,128)S(1)} %get-tuple-element.893), channel_id=1, source_target_pairs={{0,1},{1,2},{2,3},{3,4},{4,5},{5,6},{6,7},{7,0},{8,9},{9,10},{10,1... | collective-permute-start | bytes 156680 | tf_op jit(solution)/shard_map/ppermute | solution.py:16
  21.4 4.3 collective-permute-start.5
  24.8 5.1 %collective-permute-start.4 = (f32[3,1,16,128]{3,2,0,1:T(8,128)S(1)}, f32[3,1,16,128]{3,2,0,1:T(8,128)S(1)}, u32[]{:S(2)}, u32[]{:S(2)}) collective-permute-start(f32[3,1,16,128]{3,2,0,1:T(8,128)S(1)} %get-tuple-element.900), channel_id=1, source_target_pairs={{8,0},{16,8},{24,16},{32,24},{40,32},{48,40},{56,48},{64,56},{72,6... | collective-permute-start | bytes 73736 | tf_op jit(solution)/shard_map/ppermute | solution.py:19
  29.9 3.0 collective-permute-start.6
  30.0 5.2 %collective-permute-start.7 = (f32[3,34,1,128]{3,2,0,1:T(1,128)S(1)}, f32[3,34,1,128]{3,2,0,1:T(1,128)S(1)}, u32[]{:S(2)}, u32[]{:S(2)}) collective-permute-start(f32[3,34,1,128]{3,2,0,1:T(1,128)S(1)} %get-tuple-element.891), channel_id=1, source_target_pairs={{0,1},{1,2},{2,3},{3,4},{4,5},{5,6},{6,7},{7,0},{8,9},{9,10},{10,1... | collective-permute-start | bytes 156680 | tf_op jit(solution)/shard_map/ppermute | solution.py:16
  38.6 73.0 %all-to-all-start = ((f32[3,3,32,16,128]{4,3,1,0,2:T(8,128)}), f32[3,3,32,16,128]{4,3,1,0,2:T(8,128)S(1)}, u32[]{:S(2)}, u32[]{:S(2)}) async-start(f32[3,3,32,16,128]{4,3,1,0,2:T(8,128)} %pad_maximum_fusion.1), calls=%async_computation | async-start | bytes 4718592 | tf_op jit(solution)/shard_map/all_to_all | solution.py:80
  110.5 199.4 %copy-start.23 = (f32[32]{0:T(128)S(1)}, f32[32]{0:T(128)}, u32[]{:S(2)}) copy-start(f32[32]{0:T(128)} %get-tuple-element.880) | copy-start | bytes 388
  110.5 201.1 %copy-start.22 = (f32[32]{0:T(128)S(1)}, f32[32]{0:T(128)}, u32[]{:S(2)}) copy-start(f32[32]{0:T(128)} %get-tuple-element.879) | copy-start | bytes 388
  110.5 202.7 %copy-start.33 = (f32[32]{0:T(128)S(1)}, f32[32]{0:T(128)}, u32[]{:S(2)}) copy-start(f32[32]{0:T(128)} %get-tuple-element.878) | copy-start | bytes 388
  110.5 204.4 %copy-start.21 = (f32[32]{0:T(128)S(1)}, f32[32]{0:T(128)}, u32[]{:S(2)}) copy-start(f32[32]{0:T(128)} %get-tuple-element.877) | copy-start | bytes 388
  110.5 206.1 %copy-start.20 = (f32[32]{0:T(128)S(1)}, f32[32]{0:T(128)}, u32[]{:S(2)}) copy-start(f32[32]{0:T(128)} %get-tuple-element.876) | copy-start | bytes 388
  110.6 207.8 %copy-start.19 = (f32[32]{0:T(128)S(1)}, f32[32]{0:T(128)}, u32[]{:S(2)}) copy-start(f32[32]{0:T(128)} %get-tuple-element.875) | copy-start | bytes 388
  110.6 209.5 %copy-start.18 = (f32[32]{0:T(128)S(1)}, f32[32]{0:T(128)}, u32[]{:S(2)}) copy-start(f32[32]{0:T(128)} %get-tuple-element.873) | copy-start | bytes 388
  110.6 211.1 %copy-start.17 = (f32[32]{0:T(128)S(1)}, f32[32]{0:T(128)}, u32[]{:S(2)}) copy-start(f32[32]{0:T(128)} %get-tuple-element.872) | copy-start | bytes 388
  110.6 212.8 %copy-start.16 = (f32[32]{0:T(128)S(1)}, f32[32]{0:T(128)}, u32[]{:S(2)}) copy-start(f32[32]{0:T(128)} %get-tuple-element.871) | copy-start | bytes 388
  110.6 214.5 %copy-start.15 = (f32[32]{0:T(128)S(1)}, f32[32]{0:T(128)}, u32[]{:S(2)}) copy-start(f32[32]{0:T(128)} %get-tuple-element.870) | copy-start | bytes 388
  110.6 216.1 %copy-start.32 = (f32[32]{0:T(128)S(1)}, f32[32]{0:T(128)}, u32[]{:S(2)}) copy-start(f32[32]{0:T(128)} %get-tuple-element.869) | copy-start | bytes 388
  110.6 217.8 %copy-start.14 = (f32[32]{0:T(128)S(1)}, f32[32]{0:T(128)}, u32[]{:S(2)}) copy-start(f32[32]{0:T(128)} %get-tuple-element.868) | copy-start | bytes 388
  110.6 219.4 %copy-start.13 = (f32[32]{0:T(128)S(1)}, f32[32]{0:T(128)}, u32[]{:S(2)}) copy-start(f32[32]{0:T(128)} %get-tuple-element.867) | copy-start | bytes 388
  110.6 221.0 %copy-start.12 = (f32[32]{0:T(128)S(1)}, f32[32]{0:T(128)}, u32[]{:S(2)}) copy-start(f32[32]{0:T(128)} %get-tuple-element.866) | copy-start | bytes 388
  110.6 229.6 %copy-start.31 = (f32[32]{0:T(128)S(1)}, f32[32]{0:T(128)}, u32[]{:S(2)}) copy-start(f32[32]{0:T(128)} %get-tuple-element.861) | copy-start | bytes 388
  (21 other events, 1907.4 us)
where the time goes:
time: 469 us; the launch traced here: 461 us
  local copies, waits for them, and re-layouts  153 us (33%)
  matrix products  153 us (33%)
  blocking collectives  68.9 us (15%)
  other arithmetic  28.8 us (6%)
  between operations  25.7 us (5%)
  starting transfers between devices  16.9 us (4%)
  waiting for transfers between devices  14.9 us (3%)
    unnamed x79, local copies, waits for them, and re-layouts  77.9 us
    psum x1, blocking collectives, shards(): gram = lax.psum(local_gram, ('slab', 'tile'))  68.9 us
    dot_general x35, matrix products, upper_solve(): jnp.dot(factor[row_index], solved, precision=lax.Precision.HIGHEST, prefe...  48.9 us
    dot_general x1, matrix products, shards(): jnp.dot(mixing.T, columns, precision=lax.Precision.HIGHEST, preferred_ele...  48 us
    dot_general x1, matrix products, shards(): jnp.dot(columns, columns.T, precision=lax.Precision.HIGHEST, preferred_el...  28.8 us
    mul x1, local copies, waits for them, and re-layouts, shards(): scaled = basis.astype(jnp.float32) * sigma[:, None, None, None, None]  28.1 us
    dot_general x35, matrix products, upper_factor(): jnp.dot(above, factor, precision=lax.Precision.HIGHEST, preferred_element...  27.4 us
    slice x34, local copies, waits for them, and re-layouts, upper_factor(): pivot = jnp.sqrt(remainder[column_index])  20.3 us
  transfers between devices with their start and end apart: 9, of which 7 were waited for; matrix products, arithmetic and copies ran while one was open for 16% of the time, Pallas kernels for 0%

commit v1 on v0

--- a/solution.py
+++ b/solution.py
@@ -5,6 +5,11 @@
 from jax.sharding import PartitionSpec as P
 
 step_size = 0.25
+
+
+def one_after_other(value, inner_axis, outer_axis):
+    half = lax.psum(value, inner_axis)
+    return lax.psum(half, outer_axis)
 
 
 def extended(block, sides, width):
@@ -94,7 +99,7 @@
     local_gram = jnp.dot(
         columns, columns.T, precision=lax.Precision.HIGHEST, preferred_element_type=jnp.float32
     )
-    gram = lax.psum(local_gram, ("slab", "tile"))
+    gram = one_after_other(local_gram, "tile", "slab")
     factor = upper_factor(gram)
     mixing = upper_solve(factor, rotation) * row_scale
     rotated = jnp.dot(

time: 469 us -> 501 us (1.068)
  the two profiles are of different devices: /device:TPU:1 before, /device:TPU:0 now
where the time goes in v1:
time: 501 us; the launch traced here: 493 us
  local copies, waits for them, and re-layouts  153 us (31%)
  matrix products  153 us (31%)
  blocking collectives  99.5 us (20%)
  other arithmetic  28.8 us (6%)
  between operations  25.7 us (5%)
  starting transfers between devices  21.9 us (4%)
  waiting for transfers between devices  11.3 us (2%)
    unnamed x79, local copies, waits for them, and re-layouts  77.9 us
    psum x1, blocking collectives, one_after_other(): return lax.psum(half, outer_axis)  64.9 us
    dot_general x35, matrix products, upper_solve(): jnp.dot(factor[row_index], solved, precision=lax.Precision.HIGHEST, prefe...  48.9 us
    dot_general x1, matrix products, shards(): jnp.dot(mixing.T, columns, precision=lax.Precision.HIGHEST, preferred_ele...  48 us
    psum x1, blocking collectives, one_after_other(): half = lax.psum(value, inner_axis)  34.6 us
    dot_general x1, matrix products, shards(): jnp.dot(columns, columns.T, precision=lax.Precision.HIGHEST, preferred_el...  28.8 us
    mul x1, local copies, waits for them, and re-layouts, shards(): scaled = basis.astype(jnp.float32) * sigma[:, None, None, None, None]  28.1 us
    dot_general x35, matrix products, upper_factor(): jnp.dot(above, factor, precision=lax.Precision.HIGHEST, preferred_element...  27.4 us
  transfers between devices with their start and end apart: 9, of which 5 were waited for; matrix products, arithmetic and copies ran while one was open for 15% of the time, Pallas kernels for 0%

profile of v1, /device:TPU:0, one launch (start us, length us, event | category | flops | bytes accessed | tf_op | source)
XLA Modules:
  0.0 493.0 jit_solution(269705700645699836)
XLA Ops:
  1.4 5.4 %collective-permute-start = (f32[3,1,16,128]{3,2,0,1:T(8,128)S(1)}, f32[3,1,16,128]{3,2,0,1:T(8,128)S(1)}, u32[]{:S(2)}, u32[]{:S(2)}) collective-permute-start(f32[3,1,16,128]{3,2,0,1:T(8,128)S(1)} %get-tuple-element.904), channel_id=1, source_target_pairs={{8,0},{16,8},{24,16},{32,24},{40,32},{48,40},{56,48},{64,56},{72,6... | collective-permute-start | bytes 73736 | tf_op jit(solution)/shard_map/ppermute | solution.py:24
  9.6 5.2 %collective-permute-start.2 = (f32[3,34,1,128]{3,2,0,1:T(1,128)S(1)}, f32[3,34,1,128]{3,2,0,1:T(1,128)S(1)}, u32[]{:S(2)}, u32[]{:S(2)}) collective-permute-start(f32[3,34,1,128]{3,2,0,1:T(1,128)S(1)} %get-tuple-element.892), channel_id=1, source_target_pairs={{1,0},{2,1},{3,2},{4,3},{5,4},{6,5},{7,6},{0,7},{9,8},{10,9},{11,1... | collective-permute-start | bytes 156680 | tf_op jit(solution)/shard_map/ppermute | solution.py:24
  17.2 3.9 collective-permute-done.3
  21.0 1.8 multiply_add_fusion.1
  23.0 5.3 %collective-permute-start.4 = (f32[3,1,16,128]{3,2,0,1:T(8,128)S(1)}, f32[3,1,16,128]{3,2,0,1:T(8,128)S(1)}, u32[]{:S(2)}, u32[]{:S(2)}) collective-permute-start(f32[3,1,16,128]{3,2,0,1:T(8,128)S(1)} %get-tuple-element.900), channel_id=1, source_target_pairs={{8,0},{16,8},{24,16},{32,24},{40,32},{48,40},{56,48},{64,56},{72,6... | collective-permute-start | bytes 73736 | tf_op jit(solution)/shard_map/ppermute | solution.py:24
  30.3 1.7 collective-permute-start.7
  32.1 2.0 collective-permute-done.6
  34.1 2.4 collective-permute-done.7
  36.5 1.8 fusion.306
  38.3 1.6 pad_maximum_fusion.1
  39.9 3.8 all-to-all-start
  43.7 11.8 %convert_multiply_fusion = f32[32,3,4,128,128]{4,0,3,2,1:T(8,128)S(1)} fusion(bf16[32,3,4,128,128]{4,3,2,1,0:T(8,128)(2,1)} %param.147, f32[32]{0:T(128)} %param.148), kind=kLoop, calls=%fused_computation.8 | loop fusion | flops 12582912 | bytes 37748864 | tf_op jit(solution)/shard_map/mul | solution.py:97
  55.5 28.1 %copy.82 = f32[32,3,4,128,128]{4,3,2,1,0:T(8,128)} copy(f32[32,3,4,128,128]{4,0,3,2,1:T(8,128)S(1)} %convert_multiply_fusion) | data formatting | bytes 50331648 | tf_op jit(solution)/shard_map/mul | solution.py:97
  83.7 25.1 %copy.100 = f32[4,8,1536,128]{3,1,2,0:T(8,128)} copy(f32[4,8,1536,128]{3,2,1,0:T(8,128)} %bitcast.1128) | data formatting | bytes 50331648
  114.4 3.0 copy.46
  117.4 28.8 %fusion.9 = f32[35,35]{1,0:T(8,128)S(1)} fusion(f32[3,3,4,128,128]{4,0,3,2,1:T(4,128)S(1)} %bitcast.1130, f32[32,3,4,128,128]{4,0,3,2,1:T(8,128)} %copy-done.1), kind=kOutput, calls=%fused_computation.15 | convolution fusion | flops 2897018880 | bytes 27530020 | tf_op jit(solution)/shard_map/dot_general | solution.py:99
  146.2 34.6 %psum.14 = f32[35,35]{1,0:T(8,128)S(1)} all-reduce(f32[35,35]{1,0:T(8,128)S(1)} %fusion.9), channel_id=1, replica_groups=mesh['slab'=16,'tile'=8] {'tile'}, use_global_device_ids=true, to_apply=%region_0.1 | all-reduce | flops 1225 | bytes 9800 | tf_op jit(solution)/shard_map/psum | solution.py:11
  180.8 64.9 %psum.15 = f32[35,35]{1,0:T(8,128)S(1)} all-reduce(f32[35,35]{1,0:T(8,128)S(1)} %psum.14), channel_id=1, replica_groups=mesh['slab'=16,'tile'=8] {'slab'}, use_global_device_ids=true, to_apply=%region_1.2 | all-reduce | flops 1225 | bytes 9800 | tf_op jit(solution)/shard_map/psum | solution.py:12
  363.6 1.5 fusion.127
  385.5 10.1 %pad_maximum_fusion = f32[35,196608]{1,0:T(8,128)S(1)} fusion(f32[3,196608]{1,0:T(4,128)S(1)} %bitcast.1131, f32[32,196608]{1,0:T(8,128)} %bitcast.1127), kind=kLoop, calls=%fused_computation.4 | loop fusion | flops 6881280 | bytes 55050240 | tf_op jit(solution)/shard_map/concatenate | solution.py:98
  395.6 14.4 %copy.89 = f32[5,8,1536,128]{3,2,1,0:T(8,128)} copy(f32[5,8,1536,128]{3,1,2,0:T(8,128)S(1)} %bitcast.1125) | data formatting | bytes 62914560
  410.0 20.3 %slice.2142 = f32[35,1536,128]{2,1,0:T(8,128)} slice(f32[40,1536,128]{2,1,0:T(8,128)} %bitcast.1126), slice={[0:35], [0:1536], [0:128]} | slice | bytes 55050240
  430.3 48.0 %fusion.6 = bf16[32,3,4,128,128]{4,0,3,2,1:T(8,128)(2,1)S(1)} fusion(f32[3,4,128,128,35]{3,2,1,0,4:T(8,128)} %bitcast.1124, f32[35,32]{0,1:T(8,128)S(1)} %scatter.349), kind=kOutput, calls=%fused_computation.9 | convolution fusion | flops 2648704000 | bytes 40112512 | tf_op jit(solution)/shard_map/dot_general | solution.py:105
  478.3 14.5 %copy.85 = bf16[32,3,4,128,128]{4,3,2,1,0:T(8,128)(2,1)} copy(bf16[32,3,4,128,128]{4,0,3,2,1:T(8,128)(2,1)S(1)} %fusion.6) | data formatting | bytes 25165824
  (377 shorter events, 127.2 us)
Async XLA Ops:
  1.4 6.9 %collective-permute-start.1 = (f32[3,1,16,128]{3,2,0,1:T(8,128)S(1)}, f32[3,1,16,128]{3,2,0,1:T(8,128)S(1)}, u32[]{:S(2)}, u32[]{:S(2)}) collective-permute-start(f32[3,1,16,128]{3,2,0,1:T(8,128)S(1)} %get-tuple-element.905), channel_id=1, source_target_pairs={{0,8},{8,16},{16,24},{24,32},{32,40},{40,48},{48,56},{56,64},{64,7... | collective-permute-start | bytes 73736 | tf_op jit(solution)/shard_map/ppermute | solution.py:21
  1.4 8.1 %collective-permute-start = (f32[3,1,16,128]{3,2,0,1:T(8,128)S(1)}, f32[3,1,16,128]{3,2,0,1:T(8,128)S(1)}, u32[]{:S(2)}, u32[]{:S(2)}) collective-permute-start(f32[3,1,16,128]{3,2,0,1:T(8,128)S(1)} %get-tuple-element.904), channel_id=1, source_target_pairs={{8,0},{16,8},{24,16},{32,24},{40,32},{48,40},{56,48},{64,56},{72,6... | collective-permute-start | bytes 73736 | tf_op jit(solution)/shard_map/ppermute | solution.py:24
  9.6 7.6 %collective-permute-start.2 = (f32[3,34,1,128]{3,2,0,1:T(1,128)S(1)}, f32[3,34,1,128]{3,2,0,1:T(1,128)S(1)}, u32[]{:S(2)}, u32[]{:S(2)}) collective-permute-start(f32[3,34,1,128]{3,2,0,1:T(1,128)S(1)} %get-tuple-element.892), channel_id=1, source_target_pairs={{1,0},{2,1},{3,2},{4,3},{5,4},{6,5},{7,6},{0,7},{9,8},{10,9},{11,1... | collective-permute-start | bytes 156680 | tf_op jit(solution)/shard_map/ppermute | solution.py:24
  14.8 6.2 %collective-permute-start.3 = (f32[3,34,1,128]{3,2,0,1:T(1,128)S(1)}, f32[3,34,1,128]{3,2,0,1:T(1,128)S(1)}, u32[]{:S(2)}, u32[]{:S(2)}) collective-permute-start(f32[3,34,1,128]{3,2,0,1:T(1,128)S(1)} %get-tuple-element.893), channel_id=1, source_target_pairs={{0,1},{1,2},{2,3},{3,4},{4,5},{5,6},{6,7},{7,0},{8,9},{9,10},{10,1... | collective-permute-start | bytes 156680 | tf_op jit(solution)/shard_map/ppermute | solution.py:21
  22.9 6.9 %collective-permute-start.5 = (f32[3,1,16,128]{3,2,0,1:T(8,128)S(1)}, f32[3,1,16,128]{3,2,0,1:T(8,128)S(1)}, u32[]{:S(2)}, u32[]{:S(2)}) collective-permute-start(f32[3,1,16,128]{3,2,0,1:T(8,128)S(1)} %get-tuple-element.899), channel_id=1, source_target_pairs={{0,8},{8,16},{16,24},{24,32},{32,40},{40,48},{48,56},{56,64},{64,7... | collective-permute-start | bytes 73736 | tf_op jit(solution)/shard_map/ppermute | solution.py:21
  23.0 6.9 %collective-permute-start.4 = (f32[3,1,16,128]{3,2,0,1:T(8,128)S(1)}, f32[3,1,16,128]{3,2,0,1:T(8,128)S(1)}, u32[]{:S(2)}, u32[]{:S(2)}) collective-permute-start(f32[3,1,16,128]{3,2,0,1:T(8,128)S(1)} %get-tuple-element.900), channel_id=1, source_target_pairs={{8,0},{16,8},{24,16},{32,24},{40,32},{48,40},{56,48},{64,56},{72,6... | collective-permute-start | bytes 73736 | tf_op jit(solution)/shard_map/ppermute | solution.py:24
  29.9 4.2 collective-permute-start.6
  30.3 6.2 %collective-permute-start.7 = (f32[3,34,1,128]{3,2,0,1:T(1,128)S(1)}, f32[3,34,1,128]{3,2,0,1:T(1,128)S(1)}, u32[]{:S(2)}, u32[]{:S(2)}) collective-permute-start(f32[3,34,1,128]{3,2,0,1:T(1,128)S(1)} %get-tuple-element.891), channel_id=1, source_target_pairs={{0,1},{1,2},{2,3},{3,4},{4,5},{5,6},{6,7},{7,0},{8,9},{9,10},{10,1... | collective-permute-start | bytes 156680 | tf_op jit(solution)/shard_map/ppermute | solution.py:21
  39.9 73.0 %all-to-all-start = ((f32[3,3,32,16,128]{4,3,1,0,2:T(8,128)}), f32[3,3,32,16,128]{4,3,1,0,2:T(8,128)S(1)}, u32[]{:S(2)}, u32[]{:S(2)}) async-start(f32[3,3,32,16,128]{4,3,1,0,2:T(8,128)} %pad_maximum_fusion.1), calls=%async_computation | async-start | bytes 4718592 | tf_op jit(solution)/shard_map/all_to_all | solution.py:85
  111.9 230.0 %copy-start.23 = (f32[32]{0:T(128)S(1)}, f32[32]{0:T(128)}, u32[]{:S(2)}) copy-start(f32[32]{0:T(128)} %get-tuple-element.880) | copy-start | bytes 388
  111.9 231.7 %copy-start.22 = (f32[32]{0:T(128)S(1)}, f32[32]{0:T(128)}, u32[]{:S(2)}) copy-start(f32[32]{0:T(128)} %get-tuple-element.879) | copy-start | bytes 388
  111.9 233.3 %copy-start.33 = (f32[32]{0:T(128)S(1)}, f32[32]{0:T(128)}, u32[]{:S(2)}) copy-start(f32[32]{0:T(128)} %get-tuple-element.878) | copy-start | bytes 388
  111.9 235.0 %copy-start.21 = (f32[32]{0:T(128)S(1)}, f32[32]{0:T(128)}, u32[]{:S(2)}) copy-start(f32[32]{0:T(128)} %get-tuple-element.877) | copy-start | bytes 388
  111.9 236.6 %copy-start.20 = (f32[32]{0:T(128)S(1)}, f32[32]{0:T(128)}, u32[]{:S(2)}) copy-start(f32[32]{0:T(128)} %get-tuple-element.876) | copy-start | bytes 388
  111.9 238.3 %copy-start.19 = (f32[32]{0:T(128)S(1)}, f32[32]{0:T(128)}, u32[]{:S(2)}) copy-start(f32[32]{0:T(128)} %get-tuple-element.875) | copy-start | bytes 388
  111.9 240.0 %copy-start.18 = (f32[32]{0:T(128)S(1)}, f32[32]{0:T(128)}, u32[]{:S(2)}) copy-start(f32[32]{0:T(128)} %get-tuple-element.873) | copy-start | bytes 388
  111.9 241.7 %copy-start.17 = (f32[32]{0:T(128)S(1)}, f32[32]{0:T(128)}, u32[]{:S(2)}) copy-start(f32[32]{0:T(128)} %get-tuple-element.872) | copy-start | bytes 388
  111.9 243.3 %copy-start.16 = (f32[32]{0:T(128)S(1)}, f32[32]{0:T(128)}, u32[]{:S(2)}) copy-start(f32[32]{0:T(128)} %get-tuple-element.871) | copy-start | bytes 388
  111.9 245.0 %copy-start.15 = (f32[32]{0:T(128)S(1)}, f32[32]{0:T(128)}, u32[]{:S(2)}) copy-start(f32[32]{0:T(128)} %get-tuple-element.870) | copy-start | bytes 388
  112.0 246.7 %copy-start.32 = (f32[32]{0:T(128)S(1)}, f32[32]{0:T(128)}, u32[]{:S(2)}) copy-start(f32[32]{0:T(128)} %get-tuple-element.869) | copy-start | bytes 388
  112.0 248.3 %copy-start.14 = (f32[32]{0:T(128)S(1)}, f32[32]{0:T(128)}, u32[]{:S(2)}) copy-start(f32[32]{0:T(128)} %get-tuple-element.868) | copy-start | bytes 388
  112.0 250.0 %copy-start.13 = (f32[32]{0:T(128)S(1)}, f32[32]{0:T(128)}, u32[]{:S(2)}) copy-start(f32[32]{0:T(128)} %get-tuple-element.867) | copy-start | bytes 388
  112.0 251.6 %copy-start.12 = (f32[32]{0:T(128)S(1)}, f32[32]{0:T(128)}, u32[]{:S(2)}) copy-start(f32[32]{0:T(128)} %get-tuple-element.866) | copy-start | bytes 388
  112.0 260.2 %copy-start.31 = (f32[32]{0:T(128)S(1)}, f32[32]{0:T(128)}, u32[]{:S(2)}) copy-start(f32[32]{0:T(128)} %get-tuple-element.861) | copy-start | bytes 388
  (21 other events, 2183.8 us)
